TPU v7x, 512 devices: a whole 4x8x8 slice. The times are simulated.
512 devices in a mesh: seq: 64 (over z, x, core), head: 8 (over y).
Axes of the slice: x: 4, y: 8, z: 8, core: 2. Of those that a mesh axis runs over, the one named last changes fastest.
Arguments:
- queries: float32 [24576, 4096], P('seq', 'head'), may hold values from -1.75 to 1.75
- key_vectors: float32 [24576, 4096], P('seq', 'head'), may hold values from -1.75 to 1.75
- value_vectors: float32 [24576, 4096], P('seq', 'head'), may hold values from -6 to 6
- out_grad: float32 [24576, 4096], P('seq', 'head'), may hold values from -6 to 6
- norm_gain: float32 [4096], P('head'), may hold values from 0.5 to 1.5
- decay_rates: float32 [32], P('head'), may hold values from 4.0690105e-07 to 0.05
- segment_ids: int32 [24576], P('seq'), may hold values from 0 to 5, never falling along the last dimension, each value on 1 to 8192 neighbouring positions
Outputs:
- query_grad: bfloat16 [24576, 4096], P('seq', 'head')
- key_grad: bfloat16 [24576, 4096], P('seq', 'head')
- value_grad: bfloat16 [24576, 4096], P('seq', 'head')
- gain_grad: float32 [4096], P('head')
Inputs may be any that keep to these rules, and one draw needn't show every extreme that they name: `segment_ids`: segment numbers never fall along the tokens; each of the 6 segments is one run of 1 to 8192 tokens, and one has exactly 8192.
All inputs are finite; a program needn't handle non-finite values.
Results may differ from a plain program's by a relative error of at most 0.001.
Values sent between devices are 32-bit elements; how exact they have to be, the bound alone decides.
No kernel may reach another device: no remote copies, remote signals or barrier semaphores. Data moves between devices by JAX's collectives and lax.ppermute only.
A program may use at most 128 MiB of HBM per device.

v0:
```python
import jax
import jax.numpy as jnp
from jax import lax
from jax.sharding import PartitionSpec as P

HEAD_DIM = 128
PRECISE = lax.Precision.HIGHEST
EPSILON = 1e-06


def entering(part, axis, combine, identity, reverse):
    count = lax.axis_size(axis)
    place = lax.axis_index(axis)
    ahead = count - 1 - place if reverse else place
    gathered = jax.tree.map(lambda a: lax.all_gather(a, axis), part)
    state = jax.tree.map(lambda a, e: jnp.zeros_like(a) + jnp.asarray(e, a.dtype), part, identity)

    def one(lap, state):
        source = count - 1 - lap if reverse else lap
        return combine(
            state, jax.tree.map(lambda a: lax.dynamic_index_in_dim(a, source, 0, False), gathered)
        )

    return lax.fori_loop(0, ahead, one, state)


def block_tables(segs, rates):
    length = segs.shape[0]
    places = jnp.arange(length, dtype=jnp.float32)
    first_seg = segs[0]
    last_seg = segs[length - 1]
    distance = places[:, None] - places[None, :]
    causal = (distance >= 0.0) & (segs[:, None] == segs[None, :])
    weights = jnp.where(
        causal[None], jnp.exp(-rates[:, None, None] * jnp.maximum(distance, 0.0)[None]), 0.0
    )
    head_first = (segs == first_seg).astype(jnp.float32)
    tail_last = (segs == last_seg).astype(jnp.float32)
    carry_in_w = jnp.exp(-rates[None, :] * (places[:, None] + 1.0)) * head_first[:, None]
    carry_out_w = jnp.exp(-rates[None, :] * (length - 1.0 - places[:, None])) * tail_last[:, None]
    back_in = jnp.exp(-rates[None, :] * (length - places[:, None])) * tail_last[:, None]
    back_out = jnp.exp(-rates[None, :] * places[:, None]) * head_first[:, None]
    multiplier = jnp.exp(-rates * length) * (first_seg == last_seg).astype(jnp.float32)
    return (weights, carry_in_w, carry_out_w, back_in, back_out, multiplier)


def join_states(earlier, later):
    early_entry, early_exit, early_mult, early_state = earlier
    late_entry, late_exit, late_mult, late_state = later
    keep_flag = ((late_entry == early_exit) | (early_exit < 0.0) | (late_entry < 0.0)).astype(
        jnp.float32
    )
    passed = late_mult * keep_flag
    state_sum = passed[:, None, None] * early_state + late_state
    multiplier = early_mult * passed
    entry_seg = jnp.where(early_entry >= 0.0, early_entry, late_entry)
    exit_seg = jnp.where(late_exit >= 0.0, late_exit, early_exit)
    return (entry_seg, exit_seg, multiplier, state_sum)


def body(queries, key_vectors, value_vectors, out_grad, norm_gain, decay_rates, segment_ids):
    length = queries.shape[0]
    head_count = queries.shape[1] // HEAD_DIM
    features = float(head_count * HEAD_DIM * lax.axis_size("head"))
    query_rows = queries.reshape(length, head_count, HEAD_DIM)
    key_rows = key_vectors.reshape(length, head_count, HEAD_DIM)
    value_rows = value_vectors.reshape(length, head_count, HEAD_DIM)
    weights, carry_in_w, carry_out_w, back_in, back_out, multiplier = block_tables(
        segment_ids, decay_rates
    )
    first_seg = segment_ids[0:1].astype(jnp.float32)
    last_seg = segment_ids[length - 1 : length].astype(jnp.float32)
    zero_state = jnp.zeros((head_count, HEAD_DIM, HEAD_DIM), jnp.float32)
    sentinel = jnp.full((1,), -1.0, jnp.float32)
    identity = (sentinel, sentinel, jnp.ones((head_count,), jnp.float32), zero_state)
    state_loc = jnp.einsum(
        "jhd,jhe->hde", key_rows * carry_out_w[:, :, None], value_rows, precision=PRECISE
    )
    prior_sum = entering(
        (first_seg, last_seg, multiplier, state_loc), "seq", join_states, identity, False
    )
    carry_in = (
        jnp.where(prior_sum[1][0] == first_seg[0], 1.0, 0.0).astype(jnp.float32) * prior_sum[3]
    )
    scores = jnp.einsum("ihd,jhd->hij", query_rows, key_rows, precision=PRECISE) * weights
    outputs = jnp.einsum("hij,jhd->ihd", scores, value_rows, precision=PRECISE)
    outputs = outputs + carry_in_w[:, :, None] * jnp.einsum(
        "ihd,hde->ihe", query_rows, carry_in, precision=PRECISE
    )
    flat_out = outputs.reshape(length, head_count * HEAD_DIM)
    shaped = out_grad * norm_gain[None, :]
    square_part = jnp.sum(flat_out * flat_out, axis=1)
    product_part = jnp.sum(shaped * flat_out, axis=1)
    squares, product = lax.psum((square_part, product_part), "head")
    inv_rms = lax.rsqrt(squares / features + EPSILON)
    coef_rms = inv_rms**3 * (product / features)
    grad_flat = inv_rms[:, None] * shaped - coef_rms[:, None] * flat_out
    gain_part = jnp.sum(out_grad * flat_out * inv_rms[:, None], axis=0)
    gain_grad = lax.psum(gain_part, "seq")
    grad_heads = grad_flat.reshape(length, head_count, HEAD_DIM)
    mixed = jnp.einsum("ihe,jhe->hij", grad_heads, value_rows, precision=PRECISE) * weights
    query_grad = jnp.einsum("hij,jhd->ihd", mixed, key_rows, precision=PRECISE)
    query_grad = query_grad + carry_in_w[:, :, None] * jnp.einsum(
        "ihe,hde->ihd", grad_heads, carry_in, precision=PRECISE
    )
    back_loc = jnp.einsum(
        "thd,the->hde", query_rows * back_out[:, :, None], grad_heads, precision=PRECISE
    )
    later_sum = entering(
        (last_seg, first_seg, multiplier, back_loc), "seq", join_states, identity, True
    )
    carry_back = (
        jnp.where(later_sum[1][0] == last_seg[0], 1.0, 0.0).astype(jnp.float32) * later_sum[3]
    )
    key_grad = jnp.einsum("hij,ihd->jhd", mixed, query_rows, precision=PRECISE)
    key_grad = key_grad + back_in[:, :, None] * jnp.einsum(
        "jhe,hde->jhd", value_rows, carry_back, precision=PRECISE
    )
    value_grad = jnp.einsum("hij,ihe->jhe", scores, grad_heads, precision=PRECISE)
    value_grad = value_grad + back_in[:, :, None] * jnp.einsum(
        "jhd,hde->jhe", key_rows, carry_back, precision=PRECISE
    )
    width = head_count * HEAD_DIM
    return (
        query_grad.reshape(length, width).astype(jnp.bfloat16),
        key_grad.reshape(length, width).astype(jnp.bfloat16),
        value_grad.reshape(length, width).astype(jnp.bfloat16),
        gain_grad,
    )


def solution(mesh):
    return jax.shard_map(
        body,
        mesh=mesh,
        in_specs=(
            P("seq", "head"),
            P("seq", "head"),
            P("seq", "head"),
            P("seq", "head"),
            P("head"),
            P("head"),
            P("seq"),
        ),
        out_specs=(P("seq", "head"), P("seq", "head"), P("seq", "head"), P("head")),
        check_vma=False,
    )
```

profile of v0, /device:TPU:8, one launch (start us, length us, event | category | flops | bytes accessed | tf_op | source)
XLA Modules:
  0.0 1081.8 jit_solution(9144376034380852265)
XLA Ops:
  7.3 1.5 fusion.89
  10.1 2.0 compare_convert_fusion
  12.1 1.4 copy.113
  13.5 1.3 dynamic-slice
  17.0 1.6 fusion.57
  20.9 137.0 %all-reduce.3 = (f32[64]{0:T(128)}, f32[256]{0:T(256)S(1)}, f32[64]{0:T(128)}) all-reduce(f32[64]{0:T(128)S(1)} %convert_dynamic-update-slice_fusion.1, f32[256]{0:T(256)S(1)} %get-tuple-element.272, f32[64]{0:T(128)S(1)} %convert_dynamic-update-slice_fusion), channel_id=2, replica_groups=mesh['seq'=64,'head'=8] {'seq'}, use_global_device_ids=true, to_apply=%add | all-reduce | flops 384 | bytes 3072
  160.1 4.0 fusion.60
  164.1 4.0 fusion.20
  168.2 3.8 multiply_reduce_fusion.2
  171.9 16.8 %psum.21 = f32[384]{0:T(512)} all-reduce(f32[384]{0:T(512)} %get-tuple-element.274), channel_id=1, replica_groups=mesh['seq'=64,'head'=8] {'head'}, use_global_device_ids=true, to_apply=%region_3.4 | all-reduce | flops 384 | bytes 3072 | tf_op jit(solution)/shard_map/psum | solution.py:94
  188.7 2.3 copy.66
  192.3 2.2 multiply_reduce_fusion
  194.5 16.8 %psum.22 = f32[384]{0:T(512)} all-reduce(f32[384]{0:T(512)} %get-tuple-element.222), channel_id=1, replica_groups=mesh['seq'=64,'head'=8] {'head'}, use_global_device_ids=true, to_apply=%region_5.6 | all-reduce | flops 384 | bytes 3072 | tf_op jit(solution)/shard_map/psum | solution.py:94
  212.0 2.5 multiply_subtract_fusion
  214.5 2.3 copy.86
  216.8 3.2 fusion.62
  220.8 4.0 fusion.55
  224.8 3.1 fusion.14
  227.9 1.6 fusion.36
  229.5 1.9 copy.80
  231.4 474.1 %psum.23 = f32[512]{0:T(512)} all-reduce(f32[512]{0:T(512)} %get-tuple-element.221), channel_id=1, replica_groups=mesh['seq'=64,'head'=8] {'seq'}, use_global_device_ids=true, to_apply=%region_9.10 | all-reduce | flops 512 | bytes 4096 | tf_op jit(solution)/shard_map/psum | solution.py:99
  705.5 4.8 fusion.23
  710.3 3.3 fusion.17
  713.7 355.5 %while.33 = (s32[]{:T(128)}, f32[1]{0:T(128)}, f32[4,128,128]{2,1,0:T(8,128)S(1)}, s32[]{:T(128)}, f32[64,1]{0,1:T(1,128)}, /*index=5*/f32[64,4]{1,0:T(8,128)}, ...) while((s32[]{:T(128)}, f32[1]{0:T(128)}, ...), condition=%wide.region_7.8_spmd, body=%wide.region_6.7_spmd.sunk | while | flops 131090 | bytes 786751 | solution.py:24
  713.8 1.3 constant_dynamic-slice_fusion.9
  730.8 1.3 constant_dynamic-slice_fusion.9
  742.1 1.3 constant_dynamic-slice_fusion.9
  759.0 1.3 constant_dynamic-slice_fusion.9
  787.2 1.3 constant_dynamic-slice_fusion.9
  792.9 1.3 constant_dynamic-slice_fusion.9
  798.5 1.3 constant_dynamic-slice_fusion.9
  832.3 1.3 constant_dynamic-slice_fusion.9
  838.0 1.3 constant_dynamic-slice_fusion.9
  843.6 1.3 constant_dynamic-slice_fusion.9
  849.2 1.3 constant_dynamic-slice_fusion.9
  866.1 1.3 constant_dynamic-slice_fusion.9
  877.4 1.3 constant_dynamic-slice_fusion.9
  911.3 1.3 constant_dynamic-slice_fusion.9
  922.5 1.3 constant_dynamic-slice_fusion.9
  939.5 1.3 constant_dynamic-slice_fusion.9
  956.4 1.3 constant_dynamic-slice_fusion.9
  973.4 1.3 constant_dynamic-slice_fusion.9
  1001.6 1.3 constant_dynamic-slice_fusion.9
  1012.9 1.3 constant_dynamic-slice_fusion.9
  1029.8 1.3 constant_dynamic-slice_fusion.9
  1041.0 1.3 constant_dynamic-slice_fusion.9
  1069.2 1.8 fusion.34
  1071.0 1.9 copy.82
  (231 shorter events, 171.3 us)
Async XLA Ops:
  7.2 9.8 copy-start
  7.2 12.1 %copy-start.15 = (s32[384]{0:T(512)S(1)}, s32[384]{0:T(512)}, u32[]{:S(2)}) copy-start(s32[384]{0:T(512)} %param.17) | copy-start | bytes 4612
  7.2 151.4 %copy-start.12 = (f32[384,512]{1,0:T(8,128)S(1)}, f32[384,512]{1,0:T(8,128)}, u32[]{:S(2)}) copy-start(f32[384,512]{1,0:T(8,128)} %param.11) | copy-start | bytes 2359300
  7.2 160.9 %all-gather.8.cloned.1.call-start = ((), (), s32[]{:S(2)}) async-start(), calls=%async_computation | async-start | bytes 17039360 | tf_op jit(solution)/shard_map/all_gather | solution.py:15
  13.5 146.5 %copy-start.8 = (f32[384,512]{0,1:T(8,128)}, f32[384,512]{0,1:T(8,128)S(1)}, u32[]{:S(2)}) copy-start(f32[384,512]{0,1:T(8,128)S(1)} %copy.113) | copy-start | bytes 2359300
  16.3 147.8 %copy-start.16 = (f32[4]{0:T(128)}, f32[4]{0:T(128)S(1)}, u32[]{:S(2)}) copy-start(f32[4]{0:T(128)S(1)} %get-tuple-element.273) | copy-start | bytes 52
  18.6 695.1 %all-gather.10.cloned.1.call-start = ((), (), s32[]{:S(2)}) async-start(), calls=%async_computation.1 | async-start | bytes 17039360 | tf_op jit(solution)/shard_map/all_gather | solution.py:15
  159.8 4.3 copy-start.5
  191.7 0.6 copy-start.18
  220.7 4.0 copy-start.6
  220.7 4.0 copy-start.9
  220.7 4.0 copy-start.17
  224.7 4.7 copy-start.1
  224.8 3.1 copy-start.4
  224.8 3.1 copy-start.14
  705.5 4.8 copy-start.2
  705.5 4.8 copy-start.3
  705.5 4.8 copy-start.7
  710.3 358.9 %copy-start.11 = (f32[384,4,128]{0,2,1:T(8,128)S(1)}, f32[384,4,128]{0,2,1:T(8,128)}, u32[]{:S(2)}) copy-start(f32[384,4,128]{0,2,1:T(8,128)} %fusion.23) | copy-start | bytes 2359300
  713.7 355.6 %copy-start.10 = (f32[384,512]{1,0:T(8,128)S(1)}, f32[384,512]{1,0:T(8,128)}, u32[]{:S(2)}) copy-start(f32[384,512]{1,0:T(8,128)} %param.12) | copy-start | bytes 2359300
  713.7 355.6 %copy-start.13 = (f32[384,4]{0,1:T(4,128)S(1)}, f32[384,4]{0,1:T(4,128)}, u32[]{:S(2)}) copy-start(f32[384,4]{0,1:T(4,128)} %get-tuple-element.271) | copy-start | bytes 18436
Sparse Core Ops, SparseCore 0:
  18.7 110.4 all-gather.7
  220.2 444.5 all-gather.9
where the time goes:
time: 1090 us; the launch traced here: 1080 us
  blocking collectives  645 us (59%)
  loops' own time  166 us (15%)
  other arithmetic  121 us (11%)
  local copies, waits for them, and re-layouts  96.1 us (9%)
  matrix products  36.2 us (3%)
  between operations  17.8 us (2%)
    psum x1, blocking collectives, body(): gain_grad = lax.psum(gain_part, 'seq')  474 us
    another operation x2, loops' own time, entering(): return lax.fori_loop(0, ahead, one, state)  166 us
    unnamed x1, blocking collectives  137 us
    dynamic_slice x63, local copies, waits for them, and re-layouts, one(): lax.dynamic_index_in_dim(a, source, 0, False)  80 us
    add x63, other arithmetic, join_states(): state_sum = passed[:, None, None] * early_state + late_state  66.4 us
    mul x63, other arithmetic, join_states(): passed = late_mult * keep_flag  43.5 us
    psum x2, blocking collectives, body(): squares, product = lax.psum((square_part, product_part), 'head')  33.6 us
  transfers between devices with their start and end apart: 2, of which 0 were waited for; matrix products, arithmetic and copies ran while one was open for 3% of the time, Pallas kernels for 0%

commit v1 on v0

--- a/solution.py
+++ b/solution.py
@@ -96,7 +96,7 @@
     coef_rms = inv_rms**3 * (product / features)
     grad_flat = inv_rms[:, None] * shaped - coef_rms[:, None] * flat_out
     gain_part = jnp.sum(out_grad * flat_out * inv_rms[:, None], axis=0)
-    gain_grad = lax.psum(gain_part, "seq")
+    gain_grad = jnp.sum(lax.all_gather(gain_part, "seq"), axis=0)
     grad_heads = grad_flat.reshape(length, head_count, HEAD_DIM)
     mixed = jnp.einsum("ihe,jhe->hij", grad_heads, value_rows, precision=PRECISE) * weights
     query_grad = jnp.einsum("hij,jhd->ihd", mixed, key_rows, precision=PRECISE)

time: 1090 us -> 1040 us (0.954)
  blocking collectives: 645 us -> 563 us
  waiting for transfers between devices: 0.05 us -> 32.5 us
    psum x1 -> x0, blocking collectives: 474 us -> none  [body(): gain_grad = lax.psum(gain_part, 'seq')]
    all_gather x0 -> x1, blocking collectives: none -> 392 us  [body(): gain_grad = jnp.sum(lax.all_gather(gain_part, 'seq'), axis=0)]
    all_gather x2, waiting for transfers between devices: 0.02 us -> 32.4 us  [entering(): gathered = jax.tree.map(lambda a: lax.all_gather(a, axis), part)]
  transfers between devices with their start and end apart: 2 -> 2, of which waited for: 0 -> 1; matrix products, arithmetic and copies ran while one was open for 3% -> 3% of each run, Pallas kernels for 0% -> 0%
where the time goes in v1:
time: 1040 us; the launch traced here: 1030 us
  blocking collectives  563 us (54%)
  loops' own time  166 us (16%)
  other arithmetic  122 us (12%)
  local copies, waits for them, and re-layouts  95.9 us (9%)
  matrix products  35.7 us (3%)
  waiting for transfers between devices  32.5 us (3%)
  between operations  17.7 us (2%)
    all_gather x1, blocking collectives, body(): gain_grad = jnp.sum(lax.all_gather(gain_part, 'seq'), axis=0)  392 us
    another operation x2, loops' own time, entering(): return lax.fori_loop(0, ahead, one, state)  166 us
    unnamed x1, blocking collectives  137 us
    dynamic_slice x63, local copies, waits for them, and re-layouts, one(): lax.dynamic_index_in_dim(a, source, 0, False)  79.8 us
    add x63, other arithmetic, join_states(): state_sum = passed[:, None, None] * early_state + late_state  66.4 us
    mul x63, other arithmetic, join_states(): passed = late_mult * keep_flag  43.5 us
    psum x2, blocking collectives, body(): squares, product = lax.psum((square_part, product_part), 'head')  33.6 us
    all_gather x2, waiting for transfers between devices, entering(): gathered = jax.tree.map(lambda a: lax.all_gather(a, axis), part)  32.4 us
  transfers between devices with their start and end apart: 2, of which 1 were waited for; matrix products, arithmetic and copies ran while one was open for 3% of the time, Pallas kernels for 0%

profile of v1, /device:TPU:8, one launch (start us, length us, event | category | flops | bytes accessed | tf_op | source)
XLA Modules:
  0.0 1032.3 jit_solution(8861589623123865702)
XLA Ops:
  7.3 1.5 fusion.89
  10.1 2.0 compare_convert_fusion
  12.1 1.4 copy.113
  13.5 1.3 dynamic-slice
  16.9 1.6 fusion.57
  20.9 137.0 %all-reduce.3 = (f32[64]{0:T(128)}, f32[256]{0:T(256)S(1)}, f32[64]{0:T(128)}) all-reduce(f32[64]{0:T(128)S(1)} %convert_dynamic-update-slice_fusion.1, f32[256]{0:T(256)S(1)} %get-tuple-element.272, f32[64]{0:T(128)S(1)} %convert_dynamic-update-slice_fusion), channel_id=2, replica_groups=mesh['seq'=64,'head'=8] {'seq'}, use_global_device_ids=true, to_apply=%add | all-reduce | flops 384 | bytes 3072
  160.0 4.0 fusion.60
  164.1 4.0 fusion.20
  168.1 3.8 multiply_reduce_fusion.2
  171.9 16.8 %psum.14 = f32[384]{0:T(512)} all-reduce(f32[384]{0:T(512)} %get-tuple-element.274), channel_id=1, replica_groups=mesh['seq'=64,'head'=8] {'head'}, use_global_device_ids=true, to_apply=%region_3.4 | all-reduce | flops 384 | bytes 3072 | tf_op jit(solution)/shard_map/psum | solution.py:94
  188.7 2.3 copy.66
  192.3 2.2 multiply_reduce_fusion
  194.5 16.8 %psum.15 = f32[384]{0:T(512)} all-reduce(f32[384]{0:T(512)} %get-tuple-element.222), channel_id=1, replica_groups=mesh['seq'=64,'head'=8] {'head'}, use_global_device_ids=true, to_apply=%region_5.6 | all-reduce | flops 384 | bytes 3072 | tf_op jit(solution)/shard_map/psum | solution.py:94
  212.0 2.4 multiply_subtract_fusion
  214.4 2.3 copy.86
  216.7 3.2 fusion.62
  220.7 4.0 fusion.55
  224.7 3.1 fusion.14
  227.8 1.6 fusion.36
  229.4 1.9 copy.80
  231.3 392.4 %all-gather.6 = f32[64,1,512]{2,1,0:T(1,128)S(1)} all-gather(f32[1,1,512]{2,1,0:T(1,128)} %bitcast.150), channel_id=7, replica_groups=mesh['seq'=64,'head'=8] {'seq'}, dimensions={0}, use_global_device_ids=true | all-gather | bytes 133120 | tf_op jit(solution)/shard_map/all_gather | solution.py:99
  624.4 5.0 fusion.23
  629.4 2.6 fusion.17
  632.1 32.4 %all-gather.12.cloned.1.call-done = f32[256,128,128]{2,1,0:T(8,128)} async-done(((f32[4,128,128]{2,1,0:T(8,128)}), f32[256,128,128]{2,1,0:T(8,128)}) %all-gather.12.cloned.1.call-update) | async-done | bytes 16777232 | tf_op jit(solution)/shard_map/all_gather | solution.py:15
  664.5 355.2 %while.33 = (s32[]{:T(128)}, f32[1]{0:T(128)}, f32[4,128,128]{2,1,0:T(8,128)S(1)}, s32[]{:T(128)}, f32[64,1]{0,1:T(1,128)}, /*index=5*/f32[64,4]{1,0:T(8,128)}, ...) while((s32[]{:T(128)}, f32[1]{0:T(128)}, ...), condition=%wide.region_7.8_spmd, body=%wide.region_6.7_spmd.sunk | while | flops 131090 | bytes 786751 | solution.py:24
  664.6 1.3 constant_dynamic-slice_fusion.9
  670.2 1.3 constant_dynamic-slice_fusion.9
  675.8 1.3 constant_dynamic-slice_fusion.9
  681.5 1.3 constant_dynamic-slice_fusion.9
  687.1 1.3 constant_dynamic-slice_fusion.9
  692.7 1.3 constant_dynamic-slice_fusion.9
  698.4 1.3 constant_dynamic-slice_fusion.9
  704.0 1.3 constant_dynamic-slice_fusion.9
  709.6 1.3 constant_dynamic-slice_fusion.9
  715.3 1.3 constant_dynamic-slice_fusion.9
  720.9 1.3 constant_dynamic-slice_fusion.9
  726.5 1.3 constant_dynamic-slice_fusion.9
  732.2 1.3 constant_dynamic-slice_fusion.9
  737.8 1.3 constant_dynamic-slice_fusion.9
  743.5 1.3 constant_dynamic-slice_fusion.9
  749.1 1.3 constant_dynamic-slice_fusion.9
  754.7 1.3 constant_dynamic-slice_fusion.9
  788.6 1.3 constant_dynamic-slice_fusion.9
  884.5 1.3 constant_dynamic-slice_fusion.9
  918.4 1.3 constant_dynamic-slice_fusion.9
  946.6 1.3 constant_dynamic-slice_fusion.9
  1019.8 1.8 fusion.34
  1021.6 1.9 copy.82
  (234 shorter events, 173.1 us)
Async XLA Ops:
  7.2 9.8 copy-start
  7.2 12.1 %copy-start.15 = (s32[384]{0:T(512)S(1)}, s32[384]{0:T(512)}, u32[]{:S(2)}) copy-start(s32[384]{0:T(512)} %param.17) | copy-start | bytes 4612
  7.2 151.4 %copy-start.12 = (f32[384,512]{1,0:T(8,128)S(1)}, f32[384,512]{1,0:T(8,128)}, u32[]{:S(2)}) copy-start(f32[384,512]{1,0:T(8,128)} %param.11) | copy-start | bytes 2359300
  7.2 160.9 %all-gather.10.cloned.1.call-start = ((), (), s32[]{:S(2)}) async-start(), calls=%async_computation | async-start | bytes 17039360 | tf_op jit(solution)/shard_map/all_gather | solution.py:15
  13.5 146.5 %copy-start.8 = (f32[384,512]{0,1:T(8,128)}, f32[384,512]{0,1:T(8,128)S(1)}, u32[]{:S(2)}) copy-start(f32[384,512]{0,1:T(8,128)S(1)} %copy.113) | copy-start | bytes 2359300
  16.2 147.8 %copy-start.16 = (f32[4]{0:T(128)}, f32[4]{0:T(128)S(1)}, u32[]{:S(2)}) copy-start(f32[4]{0:T(128)S(1)} %get-tuple-element.273) | copy-start | bytes 52
  18.6 645.9 %all-gather.12.cloned.1.call-start = ((), (), s32[]{:S(2)}) async-start(), calls=%async_computation.1 | async-start | bytes 17039360 | tf_op jit(solution)/shard_map/all_gather | solution.py:15
  159.8 4.3 copy-start.5
  191.7 0.6 copy-start.19
  220.7 4.0 copy-start.6
  220.7 4.0 copy-start.9
  220.7 4.0 copy-start.17
  224.7 4.7 copy-start.1
  224.7 3.1 copy-start.4
  224.7 3.1 copy-start.14
  624.4 5.0 copy-start.2
  624.4 5.0 copy-start.3
  624.4 5.0 copy-start.7
  624.4 5.0 copy-start.18
  629.4 390.4 %copy-start.11 = (f32[384,4,128]{0,2,1:T(8,128)S(1)}, f32[384,4,128]{0,2,1:T(8,128)}, u32[]{:S(2)}) copy-start(f32[384,4,128]{0,2,1:T(8,128)} %fusion.23) | copy-start | bytes 2359300
  632.1 387.7 %copy-start.10 = (f32[384,512]{1,0:T(8,128)S(1)}, f32[384,512]{1,0:T(8,128)}, u32[]{:S(2)}) copy-start(f32[384,512]{1,0:T(8,128)} %param.12) | copy-start | bytes 2359300
  632.1 387.7 %copy-start.13 = (f32[384,4]{0,1:T(4,128)S(1)}, f32[384,4]{0,1:T(4,128)}, u32[]{:S(2)}) copy-start(f32[384,4]{0,1:T(4,128)} %get-tuple-element.271) | copy-start | bytes 18436
Sparse Core Ops, SparseCore 0:
  18.7 110.4 all-gather.9
  220.1 444.3 all-gather.11
